TPU v7x, 256 devices: a whole 4x4x8 slice. The times are simulated.
256 devices in a mesh: fx: 32 (over z, y), fy: 4 (over x), fz: 2 (over core).
Axes of the slice: x: 4, y: 4, z: 8, core: 2. Of those that a mesh axis runs over, the one named last changes fastest.
Arguments:
- state: float32 [5, 16, 1024, 512], P(None, 'fz', 'fx', 'fy'), may hold values from -6 to 6
- kappa: float32 [16, 1024, 512], P('fz', 'fx', 'fy'), may hold values from 0.25 to 1
- mix: float32 [5, 5], replicated, may hold values from -0.16 to 0.16
- press_weight: float32 [5], replicated, may hold values from 0.5 to 1.5
- source_weight: float32 [5], replicated, may hold values from 0.05 to 0.2
- interp: float32 [128, 128], replicated, may hold values from -0.25 to 0.25
- block_inverse: float32 [512, 128, 128], P('fx'), as said below
- coupling: float32 [512, 128, 128], P('fx'), may hold values from -0.125 to 0.125
- front_order: int32 [32, 16], P('fx'), may hold values from 0 to 15, each once within a row
- face_owner: int32 [4096, 1], P(('fx', 'fy')), may hold values from 0 to 31; in each aligned block of 32 rows (0 to 31, 32 to 63, ...) at most 2 rows name the same one
- face_slot: int32 [4096], P(('fx', 'fy')), may hold values from 0 to 15
Outputs:
- state_out: float32 [5, 16, 1024, 512], P(None, 'fz', 'fx', 'fy')
- displacement: float32 [512, 128], P('fx')
Inputs may be any that keep to these rules, and one draw needn't show every extreme that they name: `face_owner`: in the rows of one device no owner is named more than 2 times; every draw has some device naming one owner exactly 2 times. `front_order`: each row lists every block of one owner once. `block_inverse`: each block is the inverse of a stiffness block.
All inputs are finite; a program needn't handle non-finite values.
Results may differ from a plain program's by a relative error of at most 0.00021.
Values sent between devices are 32-bit elements; how exact they have to be, the bound alone decides.
A program may use at most 64 MiB of HBM per device.

v0:
```python
import jax
import jax.numpy as jnp
from jax import lax
from jax.sharding import PartitionSpec as P

ITERS = 3
DIFFUSION = 0.16
HIGHEST = lax.Precision.HIGHEST


def with_halo(cells, sides, width):
    for axis, dim in sides:
        count = lax.axis_size(axis)
        ends = count - 1
        head = lax.slice_in_dim(cells, 0, width, axis=dim)
        tail = lax.slice_in_dim(cells, cells.shape[dim] - width, cells.shape[dim], axis=dim)
        cells = jnp.concatenate(
            [
                lax.ppermute(tail, axis, [(i, (i + 1) % count) for i in range(ends)]),
                cells,
                lax.ppermute(head, axis, [((i + 1) % count, i) for i in range(ends)]),
            ],
            axis=dim,
        )
    return cells


def sweep_core(padded, coeff, mix):
    centre = padded[:, 1:-1, 1:-1, 1:-1]
    beside = padded[:, 2:, 1:-1, 1:-1] + padded[:, :-2, 1:-1, 1:-1]
    beside = beside + padded[:, 1:-1, 2:, 1:-1] + padded[:, 1:-1, :-2, 1:-1]
    beside = beside + padded[:, 1:-1, 1:-1, 2:] + padded[:, 1:-1, 1:-1, :-2]
    mixed = jnp.einsum("cd,dzxy->czxy", mix, centre, precision=HIGHEST)
    return centre + DIFFUSION * coeff[None] * (beside - 6.0 * centre) + mixed


def frontal(block_loads, inverse, coupling, order):
    blocks_owner, block_dofs = block_loads.shape

    def advance(position, carry):
        previous, solved = carry
        target = order[position]
        right_side = block_loads[target] - jnp.dot(coupling[target], previous, precision=HIGHEST)
        current = jnp.dot(inverse[target], right_side, precision=HIGHEST)
        return (current, solved.at[target].set(current))

    start = (
        jnp.zeros((block_dofs,), jnp.float32),
        jnp.zeros((blocks_owner, block_dofs), jnp.float32),
    )
    return lax.fori_loop(0, blocks_owner, advance, start)[1]


def on_device(
    state,
    kappa,
    mix,
    press_weight,
    source_weight,
    interp,
    block_inverse,
    coupling,
    front_order,
    face_owner,
    face_slot,
):
    count_z, count_x, count_y = kappa.shape
    blocks_owner = block_inverse.shape[0]
    owners = lax.axis_size("fx")
    wall_mask = (lax.axis_index("fz") == 0).astype(jnp.float32)
    total_z = count_z * lax.axis_size("fz")
    heights = (lax.axis_index("fz") * count_z + jnp.arange(count_z)).astype(jnp.float32)
    profile = 1.0 - heights / total_z
    owner_of = face_owner[:, 0]
    spread = (
        jnp.arange(owners * blocks_owner)[:, None] == (owner_of * blocks_owner + face_slot)[None, :]
    ).astype(jnp.float32)
    displacement = jnp.zeros((blocks_owner, interp.shape[1]), jnp.float32)
    for iteration in range(ITERS):
        for sweep_index in range(2):
            padded = with_halo(state, (("fx", 2), ("fy", 3), ("fz", 1)), 1)
            state = sweep_core(padded, kappa, mix)
        pressure = jnp.sum(press_weight[:, None, None] * state[:, 0], axis=0) * wall_mask
        outgoing = jnp.dot(spread, pressure, precision=HIGHEST)
        incoming = lax.all_to_all(outgoing, "fx", split_axis=0, concat_axis=0, tiled=True)
        forces = jnp.sum(incoming.reshape(owners, blocks_owner, count_y), axis=0)
        forces = lax.psum(forces, ("fy", "fz"))
        block_loads = jnp.dot(forces, interp, precision=HIGHEST)
        displacement = frontal(block_loads, block_inverse, coupling, front_order[0])
        face_disp = jnp.dot(displacement, interp.T, precision=HIGHEST)
        every_block = lax.all_gather(face_disp, "fx", axis=0, tiled=True)
        wall_disp = jnp.dot(spread.T, every_block, precision=HIGHEST)
        state = (
            state
            + source_weight[:, None, None, None]
            * profile[None, :, None, None]
            * wall_disp[None, None]
        )
    return (state, displacement)


def solution(mesh):
    return jax.shard_map(
        on_device,
        mesh=mesh,
        in_specs=(
            P(None, "fz", "fx", "fy"),
            P("fz", "fx", "fy"),
            P(),
            P(),
            P(),
            P(),
            P("fx", None, None),
            P("fx", None, None),
            P("fx", None),
            P(("fx", "fy"), None),
            P(("fx", "fy")),
        ),
        out_specs=(P(None, "fz", "fx", "fy"), P("fx", None)),
        check_vma=False,
    )
```

profile of v0, /device:TPU:8, one launch (start us, length us, event | category | flops | bytes accessed | tf_op | source)
XLA Modules:
  0.0 744.5 jit_solution(12291830759761344540)
XLA Ops:
  20.3 3.8 collective-permute-done.3
  40.5 4.8 collective-permute-done.7
  52.5 3.9 collective-permute-done.9
  60.0 4.5 collective-permute-start.11
  65.3 4.5 fusion.37
  71.9 13.9 %all-to-all-start = ((f32[32,16,128]{2,1,0:T(8,128)}), f32[32,16,128]{2,1,0:T(8,128)S(1)}, u32[]{:S(2)}, u32[]{:S(2)}) async-start(f32[32,16,128]{2,1,0:T(8,128)} %bitcast.34), calls=%async_computation | async-start | bytes 524288 | tf_op jit(solution)/shard_map/all_to_all | solution.py:85
  86.6 10.9 %all-to-all-done = f32[32,16,128]{2,1,0:T(8,128)S(1)} async-done(((f32[32,16,128]{2,1,0:T(8,128)}), f32[32,16,128]{2,1,0:T(8,128)S(1)}, u32[]{:S(2)}, u32[]{:S(2)}) %all-to-all-start) | async-done | bytes 262176 | tf_op jit(solution)/shard_map/all_to_all | solution.py:85
  97.5 12.7 %psum.21 = f32[16,128]{1,0:T(8,128)S(1)} all-reduce(f32[16,128]{1,0:T(8,128)S(1)} %reduce_sum.55), channel_id=1, replica_groups=mesh['fx'=32,'fy'=4,'fz'=2] {'fy','fz'}, use_global_device_ids=true, to_apply=%region_2.0 | all-reduce | flops 2048 | bytes 16384 | tf_op jit(solution)/shard_map/psum | solution.py:87
  110.4 97.6 %while.48 = (s32[]{:T(128)}, f32[128]{0:T(128)S(1)}, f32[16,128]{1,0:T(8,128)S(1)}, s32[16]{0:T(128)S(1)}, f32[16,128,128]{2,1,0:T(8,128)}, /*index=5*/f32[16,12...) while((s32[]{:T(128)}, f32[128]{0:T(128)S(1)}, ...), condition=%wide.region_5.0_spmd, body=%wide.region_3.0_spmd.sunk | while | flops 393486 | bytes 138424 | solution.py:51
  208.2 48.1 %all_gather.9 = f32[512,128]{1,0:T(8,128)S(1)} all-gather(f32[16,128]{1,0:T(8,128)S(1)} %fusion.129), channel_id=1, replica_groups=mesh['fx'=32,'fy'=4,'fz'=2] {'fx'}, dimensions={0}, use_global_device_ids=true | all-gather | bytes 270336 | tf_op jit(solution)/shard_map/all_gather | solution.py:91
  284.5 3.9 collective-permute-start.18
  290.4 5.4 collective-permute-done.19
  319.3 10.7 %all-to-all-start.1 = ((f32[32,16,128]{2,1,0:T(8,128)}), f32[32,16,128]{2,1,0:T(8,128)S(1)}, u32[]{:S(2)}, u32[]{:S(2)}) async-start(f32[32,16,128]{2,1,0:T(8,128)} %bitcast.38), calls=%async_computation.1 | async-start | bytes 524288 | tf_op jit(solution)/shard_map/all_to_all | solution.py:85
  329.9 11.7 %all-to-all-done.1 = f32[32,16,128]{2,1,0:T(8,128)S(1)} async-done(((f32[32,16,128]{2,1,0:T(8,128)}), f32[32,16,128]{2,1,0:T(8,128)S(1)}, u32[]{:S(2)}, u32[]{:S(2)}) %all-to-all-start.1) | async-done | bytes 262176 | tf_op jit(solution)/shard_map/all_to_all | solution.py:85
  341.7 12.7 %psum.22 = f32[16,128]{1,0:T(8,128)S(1)} all-reduce(f32[16,128]{1,0:T(8,128)S(1)} %reduce_sum.57), channel_id=1, replica_groups=mesh['fx'=32,'fy'=4,'fz'=2] {'fy','fz'}, use_global_device_ids=true, to_apply=%region_8.0 | all-reduce | flops 2048 | bytes 16384 | tf_op jit(solution)/shard_map/psum | solution.py:87
  354.6 97.6 %while.49 = (s32[]{:T(128)}, f32[128]{0:T(128)S(1)}, f32[16,128]{1,0:T(8,128)S(1)}, s32[16]{0:T(128)S(1)}, f32[16,128,128]{2,1,0:T(8,128)}, /*index=5*/f32[16,12...) while((s32[]{:T(128)}, f32[128]{0:T(128)S(1)}, ...), condition=%wide.region_11.0_spmd, body=%wide.region_9.0_spmd.sunk | while | flops 393486 | bytes 138424 | solution.py:51
  452.3 48.1 %all_gather.10 = f32[512,128]{1,0:T(8,128)S(1)} all-gather(f32[16,128]{1,0:T(8,128)S(1)} %fusion.131), channel_id=1, replica_groups=mesh['fx'=32,'fy'=4,'fz'=2] {'fx'}, dimensions={0}, use_global_device_ids=true | all-gather | bytes 270336 | tf_op jit(solution)/shard_map/all_gather | solution.py:91
  528.7 3.9 collective-permute-start.30
  534.6 5.4 collective-permute-done.31
  562.4 10.8 %all-to-all-start.2 = ((f32[32,16,128]{2,1,0:T(8,128)}), f32[32,16,128]{2,1,0:T(8,128)S(1)}, u32[]{:S(2)}, u32[]{:S(2)}) async-start(f32[32,16,128]{2,1,0:T(8,128)} %bitcast.42), calls=%async_computation.2 | async-start | bytes 524288 | tf_op jit(solution)/shard_map/all_to_all | solution.py:85
  573.2 11.7 %all-to-all-done.2 = f32[32,16,128]{2,1,0:T(8,128)S(1)} async-done(((f32[32,16,128]{2,1,0:T(8,128)}), f32[32,16,128]{2,1,0:T(8,128)S(1)}, u32[]{:S(2)}, u32[]{:S(2)}) %all-to-all-start.2) | async-done | bytes 262176 | tf_op jit(solution)/shard_map/all_to_all | solution.py:85
  585.0 12.7 %psum.23 = f32[16,128]{1,0:T(8,128)S(1)} all-reduce(f32[16,128]{1,0:T(8,128)S(1)} %reduce_sum.59), channel_id=1, replica_groups=mesh['fx'=32,'fy'=4,'fz'=2] {'fy','fz'}, use_global_device_ids=true, to_apply=%region_14.0 | all-reduce | flops 2048 | bytes 16384 | tf_op jit(solution)/shard_map/psum | solution.py:87
  597.9 97.0 %while.50 = (s32[]{:T(128)}, f32[128]{0:T(128)S(1)}, f32[16,128]{1,0:T(8,128)S(1)}, s32[16]{0:T(128)S(1)}, f32[16,128,128]{2,1,0:T(8,128)}, /*index=5*/f32[16,12...) while((s32[]{:T(128)}, f32[128]{0:T(128)S(1)}, ...), condition=%wide.region_17.0_spmd, body=%wide.region_15.0_spmd.sunk | while | flops 393486 | bytes 138424 | solution.py:51
  695.1 47.9 %all_gather.11 = f32[512,128]{1,0:T(8,128)S(1)} all-gather(f32[16,128]{1,0:T(8,128)S(1)} %fusion.133), channel_id=1, replica_groups=mesh['fx'=32,'fy'=4,'fz'=2] {'fx'}, dimensions={0}, use_global_device_ids=true | all-gather | bytes 270336 | tf_op jit(solution)/shard_map/all_gather | solution.py:91
  (448 shorter events, 356.5 us)
Async XLA Ops:
  2.2 5.9 collective-permute-start
  5.7 5.8 collective-permute-start.1
  14.6 5.1 collective-permute-start.2
  18.4 5.7 collective-permute-start.3
  34.6 5.9 collective-permute-start.6
  37.8 7.5 %collective-permute-start.7 = (f32[5,8,1,128]{3,0,2,1:T(8,128)S(1)}, f32[5,8,1,128]{3,0,2,1:T(8,128)S(1)}, u32[]{:S(2)}, u32[]{:S(2)}) collective-permute-start(f32[5,8,1,128]{3,0,2,1:T(8,128)S(1)} %get-tuple-element.528), channel_id=1, source_target_pairs={{8,0},{16,8},{24,16},{32,24},{40,32},{48,40},{56,48},{64,56},{72,6... | collective-permute-start | bytes 61448 | tf_op jit(solution)/shard_map/ppermute | solution.py:21
  50.6 5.8 collective-permute-start.9
  58.8 5.8 collective-permute-start.10
  60.0 5.2 collective-permute-start.11
  71.9 25.6 %all-to-all-start = ((f32[32,16,128]{2,1,0:T(8,128)}), f32[32,16,128]{2,1,0:T(8,128)S(1)}, u32[]{:S(2)}, u32[]{:S(2)}) async-start(f32[32,16,128]{2,1,0:T(8,128)} %bitcast.34), calls=%async_computation | async-start | bytes 524288 | tf_op jit(solution)/shard_map/all_to_all | solution.py:85
  256.8 5.9 collective-permute-start.12
  259.3 5.8 collective-permute-start.13
  268.4 5.7 collective-permute-start.15
  284.5 5.9 collective-permute-start.18
  288.5 7.4 collective-permute-start.19
  301.0 5.7 collective-permute-start.21
  319.3 22.4 %all-to-all-start.1 = ((f32[32,16,128]{2,1,0:T(8,128)}), f32[32,16,128]{2,1,0:T(8,128)S(1)}, u32[]{:S(2)}, u32[]{:S(2)}) async-start(f32[32,16,128]{2,1,0:T(8,128)} %bitcast.38), calls=%async_computation.1 | async-start | bytes 524288 | tf_op jit(solution)/shard_map/all_to_all | solution.py:85
  501.0 5.9 collective-permute-start.24
  503.5 5.8 collective-permute-start.25
  512.6 5.7 collective-permute-start.27
  528.7 5.9 collective-permute-start.30
  532.7 7.4 collective-permute-start.31
  545.2 5.7 collective-permute-start.33
  562.4 22.5 %all-to-all-start.2 = ((f32[32,16,128]{2,1,0:T(8,128)}), f32[32,16,128]{2,1,0:T(8,128)S(1)}, u32[]{:S(2)}, u32[]{:S(2)}) async-start(f32[32,16,128]{2,1,0:T(8,128)} %bitcast.42), calls=%async_computation.2 | async-start | bytes 524288 | tf_op jit(solution)/shard_map/all_to_all | solution.py:85
  (43 other events, 881.7 us)
where the time goes:
time: 752 us; the launch traced here: 744 us
  blocking collectives  182 us (24%)
  matrix products  149 us (20%)
  starting transfers between devices  118 us (16%)
  loops' own time  94.4 us (13%)
  waiting for transfers between devices  87.3 us (12%)
  local copies, waits for them, and re-layouts  64.7 us (9%)
  other arithmetic  46.7 us (6%)
    all_gather x3, blocking collectives, on_device(): every_block = lax.all_gather(face_disp, 'fx', axis=0, tiled=True)  144 us
    another operation x3, loops' own time, frontal(): return lax.fori_loop(0, blocks_owner, advance, start)[1]  94.4 us
    dot_general x48, matrix products, advance(): current = jnp.dot(inverse[target], right_side, precision=HIGHEST)  81.6 us
    ppermute x18, starting transfers between devices, with_halo(): lax.ppermute(tail, axis, [(i, (i + 1) % count) for i in range(ends)])  51.9 us
    dot_general x48, matrix products, advance(): jnp.dot(coupling[target], previous, precision=HIGHEST)  48.8 us
    ppermute x18, waiting for transfers between devices, with_halo(): lax.ppermute(head, axis, [((i + 1) % count, i) for i in range(ends)])  46.5 us
    psum x3, blocking collectives, on_device(): forces = lax.psum(forces, ('fy', 'fz'))  38 us
    another operation x48, other arithmetic  36.6 us
  transfers between devices with their start and end apart: 39, of which 21 were waited for; matrix products, arithmetic and copies ran while one was open for 1% of the time, Pallas kernels for 0%

commit v1 on v0

--- a/solution.py
+++ b/solution.py
@@ -6,6 +6,11 @@
 ITERS = 3
 DIFFUSION = 0.16
 HIGHEST = lax.Precision.HIGHEST
+
+
+def exchange_gather(x, mesh_axis, dim):
+    stack = jnp.stack([x] * lax.axis_size(mesh_axis))
+    return jnp.concatenate(lax.all_to_all(stack, mesh_axis, 0, 0), axis=dim)
 
 
 def with_halo(cells, sides, width):
@@ -88,7 +93,7 @@
         block_loads = jnp.dot(forces, interp, precision=HIGHEST)
         displacement = frontal(block_loads, block_inverse, coupling, front_order[0])
         face_disp = jnp.dot(displacement, interp.T, precision=HIGHEST)
-        every_block = lax.all_gather(face_disp, "fx", axis=0, tiled=True)
+        every_block = exchange_gather(face_disp, "fx", 0)
         wall_disp = jnp.dot(spread.T, every_block, precision=HIGHEST)
         state = (
             state

time: 752 us -> 660 us (0.88)
  blocking collectives: 182 us -> 71.1 us
  waiting for transfers between devices: 87.3 us -> 101 us
    all_gather x3 -> x0, blocking collectives: 144 us -> none  [on_device(): every_block = lax.all_gather(face_disp, 'fx', axis=0, tiled=True)]
    all_to_all x0 -> x2, blocking collectives: none -> 33.1 us  [exchange_gather(): return jnp.concatenate(lax.all_to_all(stack, mesh_axis, 0, 0), axis=dim)]
    all_to_all x0 -> x1, waiting for transfers between devices: none -> 11.5 us  [exchange_gather(): return jnp.concatenate(lax.all_to_all(stack, mesh_axis, 0, 0), axis=dim)]
  transfers between devices with their start and end apart: 39 -> 40, of which waited for: 21 -> 22; matrix products, arithmetic and copies ran while one was open for 1% -> 1% of each run, Pallas kernels for 0% -> 0%
where the time goes in v1:
time: 660 us; the launch traced here: 651 us
  matrix products  150 us (23%)
  starting transfers between devices  121 us (18%)
  waiting for transfers between devices  101 us (15%)
  loops' own time  94.4 us (14%)
  blocking collectives  71.1 us (11%)
  local copies, waits for them, and re-layouts  65.4 us (10%)
  other arithmetic  45.9 us (7%)
    another operation x3, loops' own time, frontal(): return lax.fori_loop(0, blocks_owner, advance, start)[1]  94.4 us
    dot_general x48, matrix products, advance(): current = jnp.dot(inverse[target], right_side, precision=HIGHEST)  82 us
    ppermute x18, starting transfers between devices, with_halo(): lax.ppermute(tail, axis, [(i, (i + 1) % count) for i in range(ends)])  53.6 us
    dot_general x48, matrix products, advance(): jnp.dot(coupling[target], previous, precision=HIGHEST)  48.8 us
    ppermute x18, waiting for transfers between devices, with_halo(): lax.ppermute(head, axis, [((i + 1) % count, i) for i in range(ends)])  48.2 us
    psum x3, blocking collectives, on_device(): forces = lax.psum(forces, ('fy', 'fz'))  38 us
    another operation x48, other arithmetic  36.5 us
    all_to_all x3, waiting for transfers between devices, on_device(): lax.all_to_all(outgoing, 'fx', split_axis=0, concat_axis=0, tiled=True)  35.2 us
  transfers between devices with their start and end apart: 40, of which 22 were waited for; matrix products, arithmetic and copies ran while one was open for 1% of the time, Pallas kernels for 0%

profile of v1, /device:TPU:8, one launch (start us, length us, event | category | flops | bytes accessed | tf_op | source)
XLA Modules:
  0.0 651.2 jit_solution(16397881675791273280)
XLA Ops:
  20.3 3.8 collective-permute-done.3
  40.4 4.8 collective-permute-done.7
  52.4 3.9 collective-permute-done.9
  60.0 4.5 collective-permute-start.11
  65.3 4.5 fusion.37
  71.8 13.9 %all-to-all-start = ((f32[32,16,128]{2,1,0:T(8,128)}), f32[32,16,128]{2,1,0:T(8,128)S(1)}, u32[]{:S(2)}, u32[]{:S(2)}) async-start(f32[32,16,128]{2,1,0:T(8,128)} %bitcast.34), calls=%async_computation | async-start | bytes 524288 | tf_op jit(solution)/shard_map/all_to_all | solution.py:90
  85.7 11.7 %all-to-all-done = f32[32,16,128]{2,1,0:T(8,128)S(1)} async-done(((f32[32,16,128]{2,1,0:T(8,128)}), f32[32,16,128]{2,1,0:T(8,128)S(1)}, u32[]{:S(2)}, u32[]{:S(2)}) %all-to-all-start) | async-done | bytes 262176 | tf_op jit(solution)/shard_map/all_to_all | solution.py:90
  97.5 12.7 %psum.21 = f32[16,128]{1,0:T(8,128)S(1)} all-reduce(f32[16,128]{1,0:T(8,128)S(1)} %reduce_sum.55), channel_id=1, replica_groups=mesh['fx'=32,'fy'=4,'fz'=2] {'fy','fz'}, use_global_device_ids=true, to_apply=%region_2.0 | all-reduce | flops 2048 | bytes 16384 | tf_op jit(solution)/shard_map/psum | solution.py:92
  110.4 98.6 %while.48 = (s32[]{:T(128)}, f32[128]{0:T(128)S(1)}, f32[16,128]{1,0:T(8,128)S(1)}, s32[16]{0:T(128)S(1)}, f32[16,128,128]{2,1,0:T(8,128)}, /*index=5*/f32[16,12...) while((s32[]{:T(128)}, f32[128]{0:T(128)S(1)}, ...), condition=%wide.region_5.0_spmd, body=%wide.region_3.0_spmd.sunk | while | flops 393486 | bytes 138424 | solution.py:56
  209.9 5.6 all-to-all-start.1
  215.6 11.5 %all-to-all-done.1 = f32[32,16,128]{2,1,0:T(8,128)S(1)} async-done(((f32[32,16,128]{2,1,0:T(8,128)}), f32[32,16,128]{2,1,0:T(8,128)S(1)}, u32[]{:S(2)}, u32[]{:S(2)}) %all-to-all-start.1) | async-done | bytes 262176 | tf_op jit(solution)/shard_map/all_to_all | solution.py:13
  262.1 5.6 collective-permute-done.19
  274.7 3.8 collective-permute-done.21
  291.1 9.2 %all-to-all-start.2 = ((f32[32,16,128]{2,1,0:T(8,128)}), f32[32,16,128]{2,1,0:T(8,128)S(1)}, u32[]{:S(2)}, u32[]{:S(2)}) async-start(f32[32,16,128]{2,1,0:T(8,128)} %bitcast.39), calls=%async_computation.2 | async-start | bytes 524288 | tf_op jit(solution)/shard_map/all_to_all | solution.py:90
  300.3 11.7 %all-to-all-done.2 = f32[32,16,128]{2,1,0:T(8,128)S(1)} async-done(((f32[32,16,128]{2,1,0:T(8,128)}), f32[32,16,128]{2,1,0:T(8,128)S(1)}, u32[]{:S(2)}, u32[]{:S(2)}) %all-to-all-start.2) | async-done | bytes 262176 | tf_op jit(solution)/shard_map/all_to_all | solution.py:90
  312.0 12.7 %psum.22 = f32[16,128]{1,0:T(8,128)S(1)} all-reduce(f32[16,128]{1,0:T(8,128)S(1)} %reduce_sum.57), channel_id=1, replica_groups=mesh['fx'=32,'fy'=4,'fz'=2] {'fy','fz'}, use_global_device_ids=true, to_apply=%region_8.0 | all-reduce | flops 2048 | bytes 16384 | tf_op jit(solution)/shard_map/psum | solution.py:92
  324.9 98.6 %while.49 = (s32[]{:T(128)}, f32[128]{0:T(128)S(1)}, f32[16,128]{1,0:T(8,128)S(1)}, s32[16]{0:T(128)S(1)}, f32[16,128,128]{2,1,0:T(8,128)}, /*index=5*/f32[16,12...) while((s32[]{:T(128)}, f32[128]{0:T(128)S(1)}, ...), condition=%wide.region_11.0_spmd, body=%wide.region_9.0_spmd.sunk | while | flops 393486 | bytes 138424 | solution.py:56
  423.8 16.6 %all_to_all.42 = f32[32,16,128]{2,1,0:T(8,128)S(1)} all-to-all(f32[32,16,128]{2,1,0:T(8,128)S(1)} %stack.7), channel_id=1, replica_groups=mesh['fx'=32,'fy'=4,'fz'=2] {'fx'}, dimensions={0} | all-to-all | bytes 524288 | tf_op jit(solution)/shard_map/all_to_all | solution.py:13
  475.5 5.5 collective-permute-done.31
  504.0 8.9 %all-to-all-start.4 = ((f32[32,16,128]{2,1,0:T(8,128)}), f32[32,16,128]{2,1,0:T(8,128)S(1)}, u32[]{:S(2)}, u32[]{:S(2)}) async-start(f32[32,16,128]{2,1,0:T(8,128)} %bitcast.44), calls=%async_computation.4 | async-start | bytes 524288 | tf_op jit(solution)/shard_map/all_to_all | solution.py:90
  512.9 11.7 %all-to-all-done.4 = f32[32,16,128]{2,1,0:T(8,128)S(1)} async-done(((f32[32,16,128]{2,1,0:T(8,128)}), f32[32,16,128]{2,1,0:T(8,128)S(1)}, u32[]{:S(2)}, u32[]{:S(2)}) %all-to-all-start.4) | async-done | bytes 262176 | tf_op jit(solution)/shard_map/all_to_all | solution.py:90
  524.7 12.7 %psum.23 = f32[16,128]{1,0:T(8,128)S(1)} all-reduce(f32[16,128]{1,0:T(8,128)S(1)} %reduce_sum.59), channel_id=1, replica_groups=mesh['fx'=32,'fy'=4,'fz'=2] {'fy','fz'}, use_global_device_ids=true, to_apply=%region_14.0 | all-reduce | flops 2048 | bytes 16384 | tf_op jit(solution)/shard_map/psum | solution.py:92
  537.5 95.3 %while.50 = (s32[]{:T(128)}, f32[128]{0:T(128)S(1)}, f32[16,128]{1,0:T(8,128)S(1)}, s32[16]{0:T(128)S(1)}, f32[16,128,128]{2,1,0:T(8,128)}, /*index=5*/f32[16,12...) while((s32[]{:T(128)}, f32[128]{0:T(128)S(1)}, ...), condition=%wide.region_17.0_spmd, body=%wide.region_15.0_spmd.sunk | while | flops 393486 | bytes 138424 | solution.py:56
  633.1 16.6 %all_to_all.43 = f32[32,16,128]{2,1,0:T(8,128)S(1)} all-to-all(f32[32,16,128]{2,1,0:T(8,128)S(1)} %stack.8), channel_id=1, replica_groups=mesh['fx'=32,'fy'=4,'fz'=2] {'fx'}, dimensions={0} | all-to-all | bytes 524288 | tf_op jit(solution)/shard_map/all_to_all | solution.py:13
  (454 shorter events, 363.5 us)
Async XLA Ops:
  2.2 5.9 collective-permute-start
  5.7 5.8 collective-permute-start.1
  18.4 5.7 collective-permute-start.3
  34.5 5.9 collective-permute-start.6
  37.7 7.5 %collective-permute-start.7 = (f32[5,8,1,128]{3,0,2,1:T(8,128)S(1)}, f32[5,8,1,128]{3,0,2,1:T(8,128)S(1)}, u32[]{:S(2)}, u32[]{:S(2)}) collective-permute-start(f32[5,8,1,128]{3,0,2,1:T(8,128)S(1)} %get-tuple-element.528), channel_id=1, source_target_pairs={{8,0},{16,8},{24,16},{32,24},{40,32},{48,40},{56,48},{64,56},{72,6... | collective-permute-start | bytes 61448 | tf_op jit(solution)/shard_map/ppermute | solution.py:26
  50.5 5.8 collective-permute-start.9
  58.7 5.8 collective-permute-start.10
  60.0 5.2 collective-permute-start.11
  71.8 25.6 %all-to-all-start = ((f32[32,16,128]{2,1,0:T(8,128)}), f32[32,16,128]{2,1,0:T(8,128)S(1)}, u32[]{:S(2)}, u32[]{:S(2)}) async-start(f32[32,16,128]{2,1,0:T(8,128)} %bitcast.34), calls=%async_computation | async-start | bytes 524288 | tf_op jit(solution)/shard_map/all_to_all | solution.py:90
  209.9 17.2 %all-to-all-start.1 = ((f32[32,16,128]{2,1,0:T(8,128)}), f32[32,16,128]{2,1,0:T(8,128)S(1)}, u32[]{:S(2)}, u32[]{:S(2)}) async-start(f32[32,16,128]{2,1,0:T(8,128)} %stack.6), calls=%async_computation.1 | async-start | bytes 524288 | tf_op jit(solution)/shard_map/all_to_all | solution.py:13
  227.7 5.9 collective-permute-start.12
  231.0 5.8 collective-permute-start.13
  240.0 5.7 collective-permute-start.15
  256.2 5.9 collective-permute-start.18
  259.7 7.9 %collective-permute-start.19 = (f32[5,8,1,128]{3,0,2,1:T(8,128)S(1)}, f32[5,8,1,128]{3,0,2,1:T(8,128)S(1)}, u32[]{:S(2)}, u32[]{:S(2)}) collective-permute-start(f32[5,8,1,128]{3,0,2,1:T(8,128)S(1)} %get-tuple-element.524), channel_id=1, source_target_pairs={{8,0},{16,8},{24,16},{32,24},{40,32},{48,40},{56,48},{64,56},{72,6... | collective-permute-start | bytes 61448 | tf_op jit(solution)/shard_map/ppermute | solution.py:26
  272.8 5.7 collective-permute-start.21
  291.1 20.9 %all-to-all-start.2 = ((f32[32,16,128]{2,1,0:T(8,128)}), f32[32,16,128]{2,1,0:T(8,128)S(1)}, u32[]{:S(2)}, u32[]{:S(2)}) async-start(f32[32,16,128]{2,1,0:T(8,128)} %bitcast.39), calls=%async_computation.2 | async-start | bytes 524288 | tf_op jit(solution)/shard_map/all_to_all | solution.py:90
  440.9 6.1 collective-permute-start.24
  444.3 5.8 collective-permute-start.25
  453.5 5.7 collective-permute-start.27
  469.6 5.9 collective-permute-start.30
  473.1 7.9 %collective-permute-start.31 = (f32[5,8,1,128]{3,0,2,1:T(8,128)S(1)}, f32[5,8,1,128]{3,0,2,1:T(8,128)S(1)}, u32[]{:S(2)}, u32[]{:S(2)}) collective-permute-start(f32[5,8,1,128]{3,0,2,1:T(8,128)S(1)} %get-tuple-element.520), channel_id=1, source_target_pairs={{8,0},{16,8},{24,16},{32,24},{40,32},{48,40},{56,48},{64,56},{72,6... | collective-permute-start | bytes 61448 | tf_op jit(solution)/shard_map/ppermute | solution.py:26
  486.8 5.7 collective-permute-start.33
  504.0 20.6 %all-to-all-start.4 = ((f32[32,16,128]{2,1,0:T(8,128)}), f32[32,16,128]{2,1,0:T(8,128)S(1)}, u32[]{:S(2)}, u32[]{:S(2)}) async-start(f32[32,16,128]{2,1,0:T(8,128)} %bitcast.44), calls=%async_computation.4 | async-start | bytes 524288 | tf_op jit(solution)/shard_map/all_to_all | solution.py:90
  (45 other events, 842.9 us)
